TPU v7x, 256 devices: a whole 4x4x8 slice. The times are simulated.
256 devices in a mesh: var: 2 (over z_lo), lat: 128 (over y, x, z_hi, core).
Axes of the slice: x: 4, y: 4, z: 8 (z_hi: 4, z_lo: 2; z = z_hi * 2 + z_lo), core: 2. Of those that a mesh axis runs over, the one named last changes fastest.
Arguments:
- grad_grid: bfloat16 [2, 768, 70, 1536], P('var', 'lat'), may hold values from -6 to 6
- remap: float32 [2, 70, 70], P('var'), may hold values from -0.75 to 0.75
- modes: float32 [2, 70, 70], P('var'), may hold values from -0.75 to 0.75
- balance: float32 [70, 70], replicated, may hold values from -0.75 to 0.75
- legendre: float32 [384, 768, 384], P('lat'), may hold values from -0.21875 to 0.21875
- control: float32 [2, 384, 140, 384], P('var', 'lat'), may hold values from -6 to 6
- step_size: float32 [2], P('var'), may hold values from 0.2 to 0.8
- owner_slots: int32 [384], replicated, may hold values from 0 to 383, each once
Outputs:
- updated: float32 [2, 384, 140, 384], P('var', 'lat')
- increment: bfloat16 [2, 768, 70, 1536], P('var', 'lat')
Inputs may be any that keep to these rules, and one draw needn't show every extreme that they name: `owner_slots`: each zonal wavenumber below 384 stands in exactly one owner slot; lat index d holds slots d * 3 to (d + 1) * 3 - 1.
All inputs are finite; a program needn't handle non-finite values.
Results may differ from a plain program's by a relative error of at most 0.001.
Values sent between devices are 32-bit elements; how exact they have to be, the bound alone decides.
A program may use at most 64 MiB of HBM per device.

v0:
```python
import functools
import math

import jax
import jax.numpy as jnp
from jax import lax
from jax.experimental import pallas as pl
from jax.experimental.pallas import tpu as pltpu
from jax.sharding import PartitionSpec as P

MESH = pl.DeviceIdType.MESH
f32 = jnp.float32
bf16 = jnp.bfloat16
LANES = 128
highest = lax.Precision.HIGHEST


def up(value, unit):
    return -(-value // unit) * unit


def dot(a, b, on_a, on_b, precision=None):
    return lax.dot_general(
        a, b, (((on_a,), (on_b,)), ((), ())), preferred_element_type=f32, precision=precision
    )


def halves(value):
    top = value.astype(bf16)
    return top, (value - top.astype(f32)).astype(bf16)


def cos_sin(steps, period):
    quarter = jnp.floor(steps * (4.0 / period) + 0.5)
    phi = (steps - quarter * (period / 4)) * (2.0 * math.pi / period)
    z = phi * phi
    s = phi * (1 + z * (-1 / 6 + z * (1 / 120 + z * (-1 / 5040 + z * (1 / 362880)))))
    c = 1 + z * (-1 / 2 + z * (1 / 24 + z * (-1 / 720 + z * (1 / 40320 + z * (-1 / 3628800)))))
    turn = quarter - 4 * jnp.floor(quarter * 0.25)
    odd = (turn == 1) | (turn == 3)
    cosine = jnp.where(odd, s, c)
    sine = jnp.where(odd, c, s)
    cosine = jnp.where((turn == 1) | (turn == 2), -cosine, cosine)
    sine = jnp.where((turn == 2) | (turn == 3), -sine, sine)
    return cosine, sine


def kernel(
    n, slots, rows, lev, nn, lon,
    grad_hbm, remap_ref, modes_ref, balance_ref, leg_hbm, ctrl_hbm, step_ref, owner_ref,
    upd_hbm, inc_ref,
    grad, gf, gext, gres, leg, lhl, ctrl, mnat, wave,
    send1a, send1b, recv1a, recv1b, send2a, send2b, recv2a, recv2b,
    xt, rt, xf, xa, va, hta, htb, htr, acc,
    oremap, omodes, steps, mats, amat, aop, cother, cs, ub, uown, uother, urecv,
    in_sem, send_sem, recv_sem, self_sem, swap_send, swap_recv, out_sem,
):
    me = lax.axis_index("lat")
    var = lax.axis_index("var")
    other = 1 - var
    full = rows * lev // LANES
    rest = rows * lev - full * LANES
    room = up(rest, 8)
    early = slots - 1
    pad = send1a.shape[1] // n
    high = up(lev, 8)
    columns = nn // LANES
    two = 2 * n

    barrier = pltpu.get_barrier_semaphore()

    def tell(plane, to):
        pl.semaphore_signal(barrier, inc=1, device_id=(plane, to), device_id_type=MESH)

    tell(other, me)

    @pl.loop(1, n)
    def _(k):
        to = lax.rem(me + k, n)
        tell(var, to)
        tell(other, to)

    grad_in = pltpu.make_async_copy(grad_hbm, grad, in_sem.at[0])
    grad_in.start()
    leg_in = [
        pltpu.make_async_copy(leg_hbm.at[:, :, pl.ds(LANES * j, LANES)], leg.at[j], in_sem.at[1 + j])
        for j in range(columns)
    ]
    ctrl_in = [
        pltpu.make_async_copy(
            ctrl_hbm.at[s, pl.ds(c * lev, lev), 0], ctrl.at[s, c], in_sem.at[1 + columns + 2 * s + c]
        )
        for s in range(slots)
        for c in range(2)
    ]
    for copy in ctrl_in + leg_in:
        copy.start()
    steps[var] = jnp.full(steps.shape[1:], step_ref[0], f32)

    owners = owner_ref[...].astype(f32).reshape(1, slots * n)
    mnat[...] = jnp.broadcast_to(owners, (LANES, slots * n)).T
    chunk = min(32, n)
    factor = math.sqrt(2.0 / lon)

    for s in range(slots):

        @pl.loop(0, n // chunk)
        def _(at, s=s):
            m = mnat[pl.ds(at * chunk * slots + s, chunk, stride=slots), :]
            lane = lax.broadcasted_iota(jnp.int32, (chunk, LANES), 1).astype(f32)
            turn_c, turn_s = cos_sin(m * LANES, lon)
            c, d = cos_sin(m * lane, lon)
            c = c * factor
            d = d * factor
            place = pl.ds(pl.multiple_of(s * two + at * chunk, 8), chunk)
            below = pl.ds(pl.multiple_of(s * two + n + at * chunk, 8), chunk)
            for j in range(lon // LANES):
                here = pl.ds(j * LANES, LANES)
                wave[0, place, here], wave[1, place, here] = halves(c)
                wave[0, below, here], wave[1, below, here] = halves(d)
                c, d = c * turn_c - d * turn_s, d * turn_c + c * turn_s

    grad_in.wait()
    for r in range(rows):
        gf[r * lev : (r + 1) * lev, :] = grad[r].astype(f32)
    for t in range(full):
        gext[t] = gf[t * LANES : (t + 1) * LANES, :].astype(bf16)
    for s in range(slots):
        gres[...] = jnp.zeros_like(gres)
        gres[s * room : s * room + rest, :] = gf[full * LANES : full * LANES + rest, :]
        gext[full + s] = gres[...].astype(bf16)

    def message(device, q):
        return pl.ds(pl.multiple_of(device * pad, 8), q)

    def strip(buffer, plane, q):
        return buffer.at[plane, pl.ds(q, n, stride=pad), :]

    def exchange(send, recv, q, stage):
        def to_device(plane, to, at):
            pltpu.make_async_remote_copy(
                send.at[plane, message(to, q)],
                recv.at[var, message(me, q)],
                send_sem.at[stage, at],
                recv_sem.at[stage, at],
                device_id=(plane, to),
                device_id_type=MESH,
            ).start()

        to_device(other, me, 1)

        @pl.loop(1, n)
        def _(k):
            to = lax.rem(me + k, n)
            to_device(var, to, 0)
            to_device(other, to, 1)

        own_block(send, recv, q, stage).start()

    def own_block(send, recv, q, stage):
        return pltpu.make_async_copy(
            send.at[var, message(me, q)], recv.at[var, message(me, q)], self_sem.at[stage]
        )

    def drain(buffer, q, sem):
        for at, count in enumerate((n - 1, n)):
            span = buffer.at[at, pl.ds(0, count * q)]
            pltpu.make_async_copy(span, span, sem.at[at]).wait()

    def arrived(send, recv, q, stage):
        own_block(send, recv, q, stage).wait()
        drain(recv, q, recv_sem.at[stage])

    def swap(source, target, at):
        return pltpu.make_async_remote_copy(
            source,
            target,
            swap_send.at[at],
            swap_recv.at[at],
            device_id=(other, me),
            device_id_type=MESH,
        )

    swaps = [
        swap(remap_ref, oremap, 0),
        swap(modes_ref, omodes, 1),
        swap(steps.at[var], steps.at[var], 2),
    ] + [swap(ctrl.at[s, other], cother.at[s], 3 + s) for s in range(slots)]
    returns = [swap(uother.at[s], urecv.at[s], 3 + slots + s) for s in range(slots)]

    def coefficients(s, columns_of):
        table = wave[:, s * two : (s + 1) * two, :].reshape(2 * two, lon)
        both = dot(table, columns_of, 1, 1)
        return both[:two] + both[two:]

    def to_strips(send, s, at):
        coef = coefficients(s, gext[:full].reshape(full * LANES, lon))
        for c in range(2):
            for t in range(full):
                strip(send, c, at + t)[...] = coef[
                    c * n : (c + 1) * n, t * LANES : (t + 1) * LANES
                ]

    for s in range(early):
        to_strips(send1a, s, s * full)
    left = coefficients(0, gext[full])
    for s in range(1, slots):
        left = left + coefficients(s, gext[full + s])
    for c in range(2):
        strip(send1a, c, early * full)[...] = left[c * n : (c + 1) * n]
    for copy in ctrl_in:
        copy.wait()
    pl.semaphore_wait(barrier, two - 1)
    exchange(send1a, recv1a, early * full + 1, 0)
    for copy in swaps:
        copy.start()
    to_strips(send1b, early, 0)
    exchange(send1b, recv1b, full, 1)

    for copy in leg_in:
        copy.wait()
    for s in range(slots):
        for r in range(rows):
            for j in range(columns):
                piece = leg[j, s, pl.ds(r, n, stride=rows), :]
                here = (slice(r * n, (r + 1) * n), slice(j * LANES, (j + 1) * LANES))
                lhl[(0, s) + here], lhl[(1, s) + here] = halves(piece)
    rt[...] = jnp.zeros_like(rt)
    xf[...] = jnp.zeros_like(xf)
    cs[...] = jnp.zeros_like(cs)
    amat[...] = jnp.zeros_like(amat)

    def level_operators():
        for copy in swaps[:3]:
            copy.wait_recv()
        mats[var, 0] = remap_ref[:, 0, :]
        mats[var, 1] = modes_ref[:, 0, :]
        mats[other, 0] = oremap[:, 0, :]
        mats[other, 1] = omodes[:, 0, :]
        both = balance_ref[...]
        first, second = slice(0, lev), slice(high, high + lev)
        amat[first, first] = dot(mats[0, 0], mats[0, 1], 1, 0, highest)
        amat[second, first] = dot(mats[1, 0], dot(both, mats[0, 1], 1, 0, highest), 1, 0, highest)
        amat[second, second] = dot(mats[1, 0], mats[1, 1], 1, 0, highest)
        aop[0], aop[1] = halves(amat[...].T)
        aop[2], aop[3] = halves(amat[...])

    def levels(at, value):
        top, low = halves(value)
        both = dot(aop[at : at + 2].reshape(4 * high, 2 * high), top, 1, 0)
        return both[: 2 * high] + both[2 * high :] + dot(aop[at], low, 1, 0)

    own_rows = pl.ds(pl.multiple_of(var * high, 8), lev)
    other_rows = pl.ds(pl.multiple_of(other * high, 8), lev)

    def spectral(s, recv, at, rest_t, send, to):
        for v in range(2):
            for t in range(full):
                xt[v, t * LANES : (t + 1) * LANES, :] = strip(recv, v, at + t)[...].T
            xt[v, full * LANES : full * LANES + rest, :] = rest_t[v][s * room : s * room + rest]
            for r in range(rows):
                xf[v * high : v * high + lev, r * n : (r + 1) * n] = xt[v, r * lev : (r + 1) * lev, :]
        xa[0], xa[1] = halves(xf[...])
        both = dot(xa[...].reshape(4 * high, rows * n), lhl[0, s], 1, 0)
        z = both[: 2 * high] + both[2 * high :] + dot(xa[0], lhl[1, s], 1, 0)
        mode = levels(0, z)
        swaps[3 + s].wait_recv()
        cs[own_rows] = ctrl[s, var]
        cs[other_rows] = cother[s]
        ub[: high] = jnp.broadcast_to(steps[0, :1, :1], (high, nn))
        ub[high:] = jnp.broadcast_to(steps[1, :1, :1], (high, nn))
        held = cs[...]
        fresh = held - ub[...] * (held + mode)
        ub[...] = fresh
        uown[s] = ub[own_rows]
        uother[s] = ub[other_rows]
        va[0], va[1] = halves(levels(2, fresh))
        both = dot(va[...].reshape(4 * high, nn), lhl[0, s], 1, 1)
        y = both[: 2 * high] + both[2 * high :] + dot(va[0], lhl[1, s], 1, 1)
        for v in range(2):
            for r in range(rows):
                xt[v, r * lev : (r + 1) * lev, :] = y[v * high : v * high + lev, r * n : (r + 1) * n]
            for t in range(full):
                strip(send, v, to + t)[...] = xt[v, t * LANES : (t + 1) * LANES, :].T
            rt[v, s * room : s * room + rest, :] = xt[v, full * LANES : full * LANES + rest, :]

    level_operators()
    arrived(send1a, recv1a, early * full + 1, 0)
    rest_t = [strip(recv1a, v, early * full)[...].T for v in range(2)]
    for s in range(early):
        spectral(s, recv1a, s * full, rest_t, send2a, s * full)
    exchange(send2a, recv2a, early * full, 2)
    arrived(send1b, recv1b, full, 1)
    spectral(early, recv1b, 0, rest_t, send2b, 0)
    for v in range(2):
        strip(send2b, v, full)[...] = rt[v].T
    exchange(send2b, recv2b, full + 1, 3)
    for copy in returns:
        copy.start()
    out = [
        pltpu.make_async_copy(
            uown.at[s], upd_hbm.at[s, pl.ds(var * lev, lev), 0], out_sem.at[s]
        )
        for s in range(slots)
    ] + [
        pltpu.make_async_copy(
            urecv.at[s], upd_hbm.at[s, pl.ds(other * lev, lev), 0], out_sem.at[slots + s]
        )
        for s in range(slots)
    ]
    for copy in out[:slots]:
        copy.start()

    def product(left, place):
        def on(here):
            top = wave[0, place, here]
            m = left.shape[1]
            both = dot(left[...].reshape(2 * m, left.shape[2]), top, 1, 0)
            return both[:m] + both[m:] + dot(left[0], wave[1, place, here], 1, 0)

        return on

    arrived(send2a, recv2a, early * full, 2)
    for s in range(early):
        for c in range(2):
            here = slice(s * two + c * n, s * two + (c + 1) * n)
            for t in range(full):
                place = slice(t * LANES, (t + 1) * LANES)
                hta[0, place, here], hta[1, place, here] = halves(strip(recv2a, c, s * full + t)[...].T)
    piece = 512
    whole = slice(0, full * LANES)
    for j in range(lon // piece):
        here = slice(j * piece, (j + 1) * piece)
        acc[whole, here] = product(hta, slice(0, early * two))(here)

    arrived(send2b, recv2b, full + 1, 3)
    for c in range(2):
        here = slice(c * n, (c + 1) * n)
        for t in range(full):
            place = slice(t * LANES, (t + 1) * LANES)
            htb[0, place, here], htb[1, place, here] = halves(strip(recv2b, c, t)[...].T)
        last = strip(recv2b, c, full)[...].T
        for s in range(slots):
            here = slice(s * two + c * n, s * two + (c + 1) * n)
            htr[0, :rest, here], htr[1, :rest, here] = halves(last[s * room : s * room + rest])
    for j in range(lon // piece):
        here = slice(j * piece, (j + 1) * piece)
        acc[whole, here] = acc[whole, here] + product(htb, slice(early * two, slots * two))(here)
        acc[full * LANES : full * LANES + rest, here] = product(htr, slice(0, slots * two))(here)[:rest]
    for r in range(rows):
        inc_ref[r] = acc[r * lev : (r + 1) * lev, :].astype(bf16)

    for s in range(slots):
        returns[s].wait_recv()
        out[slots + s].start()
    drain(send1a, early * full + 1, send_sem.at[0])
    drain(send1b, full, send_sem.at[1])
    drain(send2a, early * full, send_sem.at[2])
    drain(send2b, full + 1, send_sem.at[3])
    for copy in swaps + returns:
        copy.wait_send()
    for copy in out:
        copy.wait()


def local(n, grad_grid, remap, modes, balance, legendre, control, step_size, owner_slots):
    _, rows, lev, lon = grad_grid.shape
    slots, lats, nn = legendre.shape
    full = rows * lev // LANES
    rest = rows * lev - full * LANES
    assert slots * up(rest, 8) <= LANES and nn % LANES == 0 and lon % 512 == 0
    pad = up((slots - 1) * full + 1, 8)
    columns = nn // LANES
    vmem = pl.BlockSpec(memory_space=pltpu.VMEM)
    anywhere = pl.BlockSpec(memory_space=pl.ANY)
    message = pltpu.VMEM((2, n * pad, LANES), f32)
    high = up(lev, 8)
    pair = 2 * high
    units = pltpu.VMEM((slots, lev, nn), f32)
    square = pltpu.VMEM((lev, 1, lev), f32)
    dma = pltpu.SemaphoreType.DMA
    updated, increment = pl.pallas_call(
        functools.partial(kernel, n, slots, rows, lev, nn, lon),
        out_shape=(
            jax.ShapeDtypeStruct((slots, 2 * lev, 1, nn), f32),
            jax.ShapeDtypeStruct((rows, lev, lon), bf16),
        ),
        in_specs=[
            anywhere, vmem, vmem, vmem, anywhere, anywhere,
            pl.BlockSpec(memory_space=pltpu.SMEM), vmem,
        ],
        out_specs=(anywhere, vmem),
        scratch_shapes=[
            pltpu.VMEM((rows, lev, lon), bf16),
            pltpu.VMEM((up(rows * lev, 8), lon), f32),
            pltpu.VMEM((full + slots, LANES, lon), bf16),
            pltpu.VMEM((LANES, lon), f32),
            pltpu.VMEM((columns, slots, lats, LANES), f32),
            pltpu.VMEM((2, slots, lats, nn), bf16),
            pltpu.VMEM((slots, 2, lev, nn), f32),
            pltpu.VMEM((slots * n, LANES), f32),
            pltpu.VMEM((2, slots * 2 * n, lon), bf16),
            message, message, message, message, message, message, message, message,
            pltpu.VMEM((2, up(rows * lev, 8), n), f32),
            pltpu.VMEM((2, LANES, n), f32),
            pltpu.VMEM((pair, rows * n), f32),
            pltpu.VMEM((2, pair, rows * n), bf16),
            pltpu.VMEM((2, pair, nn), bf16),
            pltpu.VMEM((2, full * LANES, (slots - 1) * 2 * n), bf16),
            pltpu.VMEM((2, full * LANES, 2 * n), bf16),
            pltpu.VMEM((2, up(rest, 16), slots * 2 * n), bf16),
            pltpu.VMEM((up(rows * lev, 8), lon), f32),
            square, square,
            pltpu.VMEM((2, 8, LANES), f32),
            pltpu.VMEM((2, 2, lev, lev), f32),
            pltpu.VMEM((pair, pair), f32),
            pltpu.VMEM((4, pair, pair), bf16),
            units,
            pltpu.VMEM((pair, nn), f32),
            pltpu.VMEM((pair, nn), f32),
            units, units, units,
            dma((1 + columns + 2 * slots,)),
            dma((4, 2)), dma((4, 2)), dma((4,)),
            dma((3 + 2 * slots,)), dma((3 + 2 * slots,)), dma((2 * slots,)),
        ],
        compiler_params=pltpu.CompilerParams(
            collective_id=0, has_side_effects=True, vmem_limit_bytes=60 * 1024 * 1024
        ),
        name="step",
    )(
        grad_grid[0],
        jnp.transpose(remap, (1, 0, 2)),
        jnp.transpose(modes, (1, 0, 2)),
        balance,
        legendre,
        jnp.transpose(control, (1, 2, 0, 3)),
        step_size,
        owner_slots,
    )
    return jnp.transpose(updated, (2, 0, 1, 3)), increment[None]


def solution(mesh):
    return jax.shard_map(
        functools.partial(local, mesh.shape["lat"]),
        mesh=mesh,
        in_specs=(
            P("var", "lat", None, None),
            P("var", None, None),
            P("var", None, None),
            P(),
            P("lat", None, None),
            P("var", "lat", None, None),
            P("var"),
            P(),
        ),
        out_specs=(P("var", "lat", None, None), P("var", "lat", None, None)),
        check_vma=False,
    )
```

profile of v0, /device:TPU:1, one launch (start us, length us, event | category | flops | bytes accessed | tf_op | source)
XLA Modules:
  0.0 96.9 jit_solution(16157365227533677953)
XLA Ops:
  1.3 90.8 %step.1 = (f32[3,140,1,384]{3,2,1,0:T(1,128)}, bf16[6,70,1536]{2,1,0:T(8,128)(2,1)}) custom-call(bf16[6,70,1536]{2,1,0:T(8,128)(2,1)} %bitcast.7, f32[70,1,70]{2,1,0:T(1,128)} %bitcast.10, f32[70,1,70]{2,1,0:T(1,128)} %bitcast.11, f32[70,70]{1,0:T(8,128)} %balance_ref.1, f32[3,768,384]{2,1,0:T(8,128)} %leg_hbm.1, f32[3,140,1,384]{3,2,1,0:T(1,128)} %bitcast.9, ...), custom_call_target="tpu_custom_call" | custom-call | tf_op jit(solution)/shard_map/step/pallas_call | solution.py:382
  92.1 2.4 %copy.13 = f32[1,3,140,384]{3,0,2,1:T(1,128)} copy(f32[1,3,140,384]{3,0,2,1:T(1,128)} %bitcast.8) | data formatting | bytes 1290240
  94.5 2.5 %copy.14 = bf16[1,6,70,1536]{3,2,1,0:T(8,128)(2,1)} copy(bf16[1,6,70,1536]{3,2,1,0:T(8,128)(2,1)} %bitcast.6) | data formatting | bytes 2580480
where the time goes:
time: 97.2 us; the launch traced here: 96.9 us
  Pallas kernels  90.8 us (93%)
  local copies, waits for them, and re-layouts  4.83 us (5%)
  between operations  1.29 us (1%)
    pallas_call x1, Pallas kernels, local(): pl.pallas_call(functools.partial(kernel, n, slots, rows, lev, nn, lon), o...  90.8 us
    unnamed x2, local copies, waits for them, and re-layouts  4.83 us

commit v1 on v0

--- a/solution.py
+++ b/solution.py
@@ -47,13 +47,14 @@
 
 def kernel(
     n, slots, rows, lev, nn, lon,
-    grad_hbm, remap_ref, modes_ref, balance_ref, leg_hbm, ctrl_hbm, step_ref, owner_ref,
+    grad_hbm, remap_hbm, modes_hbm, balance_hbm, leg_hbm, ctrl_hbm, step_ref, owner_hbm,
     upd_hbm, inc_ref,
-    grad, gf, gext, gres, leg, lhl, ctrl, mnat, wave,
+    grad, gf, gext, leg, lhl, ctrl, mnat, wave,
     send1a, send1b, recv1a, recv1b, send2a, send2b, recv2a, recv2b,
     xt, rt, xf, xa, va, hta, htb, htr, acc,
     oremap, omodes, steps, mats, amat, aop, cother, cs, ub, uown, uother, urecv,
-    in_sem, send_sem, recv_sem, self_sem, swap_send, swap_recv, out_sem,
+    owner_ref, remap_ref, modes_ref, balance_ref,
+    small_sem, in_sem, send_sem, recv_sem, self_sem, swap_send, swap_recv, out_sem,
 ):
     me = lax.axis_index("lat")
     var = lax.axis_index("var")
@@ -68,17 +69,53 @@
     two = 2 * n
 
     barrier = pltpu.get_barrier_semaphore()
+    small_in = [
+        pltpu.make_async_copy(source, target, small_sem.at[at])
+        for at, (source, target) in enumerate(
+            (
+                (owner_hbm, owner_ref),
+                (remap_hbm, remap_ref),
+                (modes_hbm, modes_ref),
+                (balance_hbm, balance_ref),
+            )
+        )
+    ]
 
     def tell(plane, to):
         pl.semaphore_signal(barrier, inc=1, device_id=(plane, to), device_id_type=MESH)
 
-    tell(other, me)
-
-    @pl.loop(1, n)
-    def _(k):
-        to = lax.rem(me + k, n)
-        tell(var, to)
-        tell(other, to)
+    for copy in small_in:
+        copy.start()
+
+    def everywhere(act):
+        group = 8 if n % 8 == 0 else 2
+        outer = n // group
+
+        @pl.loop(0, outer)
+        def _(q):
+            if outer == 16:
+                y, x = q // 4, lax.rem(q, 4)
+                y = lax.rem(2 + 3 * y + 3 * (y // 2) + 2 * (y // 3), 4)
+                x = lax.rem(2 + 3 * x + 3 * (x // 2) + 2 * (x // 3), 4)
+                row = me // group
+                row = lax.rem(row // 4 + y, 4) * 4 + lax.rem(lax.rem(row, 4) + x, 4)
+            else:
+                row = lax.rem(me // group + outer - 1 - q, outer)
+            inner = lax.rem(me, group)
+            for z in (2, 1, 3, 0) if group == 8 else (0,):
+                for core in (1, 0):
+                    to = row * group
+                    to += lax.rem(inner // 2 + z, group // 2) * 2 + lax.rem(inner + core, 2)
+                    act(other, to, 1)
+                    if z == 0 and core == 0:
+
+                        @pl.when(q < outer - 1)
+                        def _(to=to):
+                            act(var, to, 0)
+                    else:
+                        act(var, to, 0)
+
+    everywhere(lambda plane, to, at: tell(plane, to))
 
     grad_in = pltpu.make_async_copy(grad_hbm, grad, in_sem.at[0])
     grad_in.start()
@@ -97,6 +134,7 @@
         copy.start()
     steps[var] = jnp.full(steps.shape[1:], step_ref[0], f32)
 
+    small_in[0].wait()
     owners = owner_ref[...].astype(f32).reshape(1, slots * n)
     mnat[...] = jnp.broadcast_to(owners, (LANES, slots * n)).T
     chunk = min(32, n)
@@ -123,12 +161,9 @@
     grad_in.wait()
     for r in range(rows):
         gf[r * lev : (r + 1) * lev, :] = grad[r].astype(f32)
-    for t in range(full):
+    gf[rows * lev :, :] = jnp.zeros((gf.shape[0] - rows * lev, lon), f32)
+    for t in range(full + 1):
         gext[t] = gf[t * LANES : (t + 1) * LANES, :].astype(bf16)
-    for s in range(slots):
-        gres[...] = jnp.zeros_like(gres)
-        gres[s * room : s * room + rest, :] = gf[full * LANES : full * LANES + rest, :]
-        gext[full + s] = gres[...].astype(bf16)
 
     def message(device, q):
         return pl.ds(pl.multiple_of(device * pad, 8), q)
@@ -147,15 +182,8 @@
                 device_id_type=MESH,
             ).start()
 
-        to_device(other, me, 1)
-
-        @pl.loop(1, n)
-        def _(k):
-            to = lax.rem(me + k, n)
-            to_device(var, to, 0)
-            to_device(other, to, 1)
-
         own_block(send, recv, q, stage).start()
+        everywhere(to_device)
 
     def own_block(send, recv, q, stage):
         return pltpu.make_async_copy(
@@ -188,33 +216,34 @@
     ] + [swap(ctrl.at[s, other], cother.at[s], 3 + s) for s in range(slots)]
     returns = [swap(uother.at[s], urecv.at[s], 3 + slots + s) for s in range(slots)]
 
-    def coefficients(s, columns_of):
+    def coefficients(s, first, last):
         table = wave[:, s * two : (s + 1) * two, :].reshape(2 * two, lon)
-        both = dot(table, columns_of, 1, 1)
+        both = dot(table, gext[first:last].reshape((last - first) * LANES, lon), 1, 1)
         return both[:two] + both[two:]
 
-    def to_strips(send, s, at):
-        coef = coefficients(s, gext[:full].reshape(full * LANES, lon))
+    def to_strips(send, coef, at):
         for c in range(2):
             for t in range(full):
                 strip(send, c, at + t)[...] = coef[
                     c * n : (c + 1) * n, t * LANES : (t + 1) * LANES
                 ]
 
+    left = coefficients(early, full, full + 1)
+    left = pltpu.roll(left, early * room, 1)
     for s in range(early):
-        to_strips(send1a, s, s * full)
-    left = coefficients(0, gext[full])
-    for s in range(1, slots):
-        left = left + coefficients(s, gext[full + s])
+        coef = coefficients(s, 0, full + 1)
+        to_strips(send1a, coef, s * full)
+        term = coef[:, full * LANES :]
+        left = left + (pltpu.roll(term, s * room, 1) if s else term)
     for c in range(2):
         strip(send1a, c, early * full)[...] = left[c * n : (c + 1) * n]
-    for copy in ctrl_in:
+    for copy in ctrl_in + small_in[1:]:
         copy.wait()
     pl.semaphore_wait(barrier, two - 1)
     exchange(send1a, recv1a, early * full + 1, 0)
     for copy in swaps:
         copy.start()
-    to_strips(send1b, early, 0)
+    to_strips(send1b, coefficients(early, 0, full), 0)
     exchange(send1b, recv1b, full, 1)
 
     for copy in leg_in:
@@ -373,12 +402,14 @@
     columns = nn // LANES
     vmem = pl.BlockSpec(memory_space=pltpu.VMEM)
     anywhere = pl.BlockSpec(memory_space=pl.ANY)
+    hbm = pl.BlockSpec(memory_space=pltpu.HBM)
     message = pltpu.VMEM((2, n * pad, LANES), f32)
     high = up(lev, 8)
     pair = 2 * high
     units = pltpu.VMEM((slots, lev, nn), f32)
     square = pltpu.VMEM((lev, 1, lev), f32)
     dma = pltpu.SemaphoreType.DMA
+    outside = functools.partial(pltpu.with_memory_space_constraint, memory_space=pltpu.HBM)
     updated, increment = pl.pallas_call(
         functools.partial(kernel, n, slots, rows, lev, nn, lon),
         out_shape=(
@@ -386,15 +417,14 @@
             jax.ShapeDtypeStruct((rows, lev, lon), bf16),
         ),
         in_specs=[
-            anywhere, vmem, vmem, vmem, anywhere, anywhere,
-            pl.BlockSpec(memory_space=pltpu.SMEM), vmem,
+            hbm, hbm, hbm, hbm, hbm, hbm,
+            pl.BlockSpec(memory_space=pltpu.SMEM), hbm,
         ],
         out_specs=(anywhere, vmem),
         scratch_shapes=[
             pltpu.VMEM((rows, lev, lon), bf16),
-            pltpu.VMEM((up(rows * lev, 8), lon), f32),
-            pltpu.VMEM((full + slots, LANES, lon), bf16),
-            pltpu.VMEM((LANES, lon), f32),
+            pltpu.VMEM(((full + 1) * LANES, lon), f32),
+            pltpu.VMEM((full + 1, LANES, lon), bf16),
             pltpu.VMEM((columns, slots, lats, LANES), f32),
             pltpu.VMEM((2, slots, lats, nn), bf16),
             pltpu.VMEM((slots, 2, lev, nn), f32),
@@ -419,23 +449,26 @@
             pltpu.VMEM((pair, nn), f32),
             pltpu.VMEM((pair, nn), f32),
             units, units, units,
+            pltpu.VMEM(owner_slots.shape, jnp.int32),
+            square, square, pltpu.VMEM((lev, lev), f32),
+            dma((4,)),
             dma((1 + columns + 2 * slots,)),
             dma((4, 2)), dma((4, 2)), dma((4,)),
             dma((3 + 2 * slots,)), dma((3 + 2 * slots,)), dma((2 * slots,)),
         ],
         compiler_params=pltpu.CompilerParams(
-            collective_id=0, has_side_effects=True, vmem_limit_bytes=60 * 1024 * 1024
+            collective_id=0, has_side_effects=True, vmem_limit_bytes=48 * 1024 * 1024
         ),
         name="step",
     )(
-        grad_grid[0],
-        jnp.transpose(remap, (1, 0, 2)),
-        jnp.transpose(modes, (1, 0, 2)),
-        balance,
-        legendre,
-        jnp.transpose(control, (1, 2, 0, 3)),
+        outside(grad_grid[0]),
+        outside(jnp.transpose(remap, (1, 0, 2))),
+        outside(jnp.transpose(modes, (1, 0, 2))),
+        outside(balance),
+        outside(legendre),
+        outside(jnp.transpose(control, (1, 2, 0, 3))),
         step_size,
-        owner_slots,
+        outside(owner_slots),
     )
     return jnp.transpose(updated, (2, 0, 1, 3)), increment[None]
 

time: 97.2 us -> 91.5 us (0.941)
  local copies, waits for them, and re-layouts: 4.83 us -> 1.9 us
  Pallas kernels: 90.8 us -> 88.2 us
    unnamed x2, local copies, waits for them, and re-layouts: 4.83 us -> 1.9 us
    pallas_call x1, Pallas kernels: 90.8 us -> 88.2 us  [local(): pl.pallas_call(functools.partial(kernel, n, slots, rows, lev, nn, lon), o...]
where the time goes in v1:
time: 91.5 us; the launch traced here: 91.4 us
  Pallas kernels  88.2 us (96%)
  local copies, waits for them, and re-layouts  1.9 us (2%)
  between operations  1.29 us (1%)
    pallas_call x1, Pallas kernels, local(): pl.pallas_call(functools.partial(kernel, n, slots, rows, lev, nn, lon), o...  88.2 us
    unnamed x2, local copies, waits for them, and re-layouts  1.9 us

profile of v1, /device:TPU:1, one launch (start us, length us, event | category | flops | bytes accessed | tf_op | source)
XLA Modules:
  0.0 91.4 jit_solution(13343163241457821224)
XLA Ops:
  1.3 88.2 %step.1 = (f32[3,140,1,384]{3,2,1,0:T(1,128)S(1)}, bf16[6,70,1536]{2,1,0:T(8,128)(2,1)S(1)}) custom-call(bf16[6,70,1536]{2,1,0:T(8,128)(2,1)} %bitcast.8, f32[70,1,70]{2,1,0:T(1,128)} %bitcast.10, f32[70,1,70]{2,1,0:T(1,128)} %bitcast.11, f32[70,70]{1,0:T(8,128)} %balance_hbm.1, f32[3,768,384]{2,1,0:T(8,128)} %leg_hbm.1, f32[3,140,1,384]{3,2,1,0:T(1,128)} %bitcast.9, ...), custom_call_target="tpu_custom_call" | custom-call | tf_op jit(solution)/shard_map/step/pallas_call | solution.py:413
  89.5 0.8 copy.13
  90.4 1.1 %copy.14 = bf16[1,6,70,1536]{3,2,1,0:T(8,128)(2,1)} copy(bf16[1,6,70,1536]{3,2,1,0:T(8,128)(2,1)S(1)} %bitcast.6) | data formatting | bytes 2580480

commit v2 on v1

--- a/solution.py
+++ b/solution.py
@@ -48,13 +48,13 @@
 def kernel(
     n, slots, rows, lev, nn, lon,
     grad_hbm, remap_hbm, modes_hbm, balance_hbm, leg_hbm, ctrl_hbm, step_ref, owner_hbm,
-    upd_hbm, inc_ref,
+    uown, urecv, inc_ref,
     grad, gf, gext, leg, lhl, ctrl, mnat, wave,
     send1a, send1b, recv1a, recv1b, send2a, send2b, recv2a, recv2b,
     xt, rt, xf, xa, va, hta, htb, htr, acc,
-    oremap, omodes, steps, mats, amat, aop, cother, cs, ub, uown, uother, urecv,
+    oremap, omodes, steps, mats, amat, aop, cother, cs, ub, uother,
     owner_ref, remap_ref, modes_ref, balance_ref,
-    small_sem, in_sem, send_sem, recv_sem, self_sem, swap_send, swap_recv, out_sem,
+    small_sem, in_sem, send_sem, recv_sem, self_sem, swap_send, swap_recv,
 ):
     me = lax.axis_index("lat")
     var = lax.axis_index("var")
@@ -87,11 +87,16 @@
     for copy in small_in:
         copy.start()
 
-    def everywhere(act):
-        group = 8 if n % 8 == 0 else 2
-        outer = n // group
-
-        @pl.loop(0, outer)
+    group = 8 if n % 8 == 0 else 2
+    outer = n // group
+    blocks = 4 if outer == 16 else 1
+    width = n // blocks
+
+    def far_first(digit):
+        return (2 + 3 * digit + 3 * (digit // 2) + 2 * (digit // 3)) % 4
+
+    def everywhere(act, first=0, last=outer, skip=None):
+        @pl.loop(first, last)
         def _(q):
             if outer == 16:
                 y, x = q // 4, lax.rem(q, 4)
@@ -106,8 +111,18 @@
                 for core in (1, 0):
                     to = row * group
                     to += lax.rem(inner // 2 + z, group // 2) * 2 + lax.rem(inner + core, 2)
+                    here = z == 0 and core == 0
+                    if skip is not None:
+                        if here:
+
+                            @pl.when(jnp.logical_not(skip) | (q < outer - 1))
+                            def _(to=to):
+                                act(to)
+                        else:
+                            act(to)
+                        continue
                     act(other, to, 1)
-                    if z == 0 and core == 0:
+                    if here:
 
                         @pl.when(q < outer - 1)
                         def _(to=to):
@@ -115,7 +130,13 @@
                     else:
                         act(var, to, 0)
 
-    everywhere(lambda plane, to, at: tell(plane, to))
+    hub = lax.rem(var + me, 2) == 0
+
+    @pl.when(hub)
+    def _():
+        tell(other, me)
+
+    everywhere(lambda to: tell(lax.rem(to, 2), to), skip=hub)
 
     grad_in = pltpu.make_async_copy(grad_hbm, grad, in_sem.at[0])
     grad_in.start()
@@ -158,6 +179,32 @@
                 wave[0, below, here], wave[1, below, here] = halves(d)
                 c, d = c * turn_c - d * turn_s, d * turn_c + c * turn_s
 
+    def swap(source, target, at):
+        return pltpu.make_async_remote_copy(
+            source,
+            target,
+            swap_send.at[at],
+            swap_recv.at[at],
+            device_id=(other, me),
+            device_id_type=MESH,
+        )
+
+    swaps = [
+        swap(remap_ref, oremap, 0),
+        swap(modes_ref, omodes, 1),
+        swap(steps.at[var], steps.at[var], 2),
+    ] + [swap(ctrl.at[s, other], cother.at[s], 3 + s) for s in range(slots)]
+    returns = [swap(uother.at[s], urecv.at[s], 3 + slots + s) for s in range(slots)]
+
+    for copy in ctrl_in + small_in[1:]:
+        copy.wait()
+
+    @pl.when(jnp.logical_not(hub))
+    def _():
+        pl.semaphore_wait(barrier, 1)
+        for copy in swaps:
+            copy.start()
+
     grad_in.wait()
     for r in range(rows):
         gf[r * lev : (r + 1) * lev, :] = grad[r].astype(f32)
@@ -171,7 +218,7 @@
     def strip(buffer, plane, q):
         return buffer.at[plane, pl.ds(q, n, stride=pad), :]
 
-    def exchange(send, recv, q, stage):
+    def exchange(send, recv, q, stage, blocks_done=None):
         def to_device(plane, to, at):
             pltpu.make_async_remote_copy(
                 send.at[plane, message(to, q)],
@@ -182,8 +229,13 @@
                 device_id_type=MESH,
             ).start()
 
-        own_block(send, recv, q, stage).start()
-        everywhere(to_device)
+        if blocks_done is None:
+            own_block(send, recv, q, stage).start()
+            everywhere(to_device)
+        else:
+            everywhere(to_device, blocks_done * (outer // blocks), (blocks_done + 1) * (outer // blocks))
+            if blocks_done == blocks - 1:
+                own_block(send, recv, q, stage).start()
 
     def own_block(send, recv, q, stage):
         return pltpu.make_async_copy(
@@ -198,23 +250,6 @@
     def arrived(send, recv, q, stage):
         own_block(send, recv, q, stage).wait()
         drain(recv, q, recv_sem.at[stage])
-
-    def swap(source, target, at):
-        return pltpu.make_async_remote_copy(
-            source,
-            target,
-            swap_send.at[at],
-            swap_recv.at[at],
-            device_id=(other, me),
-            device_id_type=MESH,
-        )
-
-    swaps = [
-        swap(remap_ref, oremap, 0),
-        swap(modes_ref, omodes, 1),
-        swap(steps.at[var], steps.at[var], 2),
-    ] + [swap(ctrl.at[s, other], cother.at[s], 3 + s) for s in range(slots)]
-    returns = [swap(uother.at[s], urecv.at[s], 3 + slots + s) for s in range(slots)]
 
     def coefficients(s, first, last):
         table = wave[:, s * two : (s + 1) * two, :].reshape(2 * two, lon)
@@ -228,21 +263,57 @@
                     c * n : (c + 1) * n, t * LANES : (t + 1) * LANES
                 ]
 
-    left = coefficients(early, full, full + 1)
-    left = pltpu.roll(left, early * room, 1)
-    for s in range(early):
-        coef = coefficients(s, 0, full + 1)
-        to_strips(send1a, coef, s * full)
-        term = coef[:, full * LANES :]
-        left = left + (pltpu.roll(term, s * room, 1) if s else term)
-    for c in range(2):
-        strip(send1a, c, early * full)[...] = left[c * n : (c + 1) * n]
-    for copy in ctrl_in + small_in[1:]:
-        copy.wait()
-    pl.semaphore_wait(barrier, two - 1)
-    exchange(send1a, recv1a, early * full + 1, 0)
-    for copy in swaps:
-        copy.start()
+    def block_table(s, start):
+        return [
+            wave[half, pl.ds(pl.multiple_of(s * two + c * n + start, 8), width), :]
+            for half in range(2)
+            for c in range(2)
+        ]
+
+    for block in range(blocks):
+        start = 0
+        if blocks == 4:
+            start = lax.rem(me // width + far_first(block), blocks) * width
+        tables = sum([block_table(s, start) for s in range(early)], [])
+        main = dot(
+            jnp.concatenate(tables, axis=0), gext[...].reshape((full + 1) * LANES, lon), 1, 1
+        )
+        last = dot(jnp.concatenate(block_table(early, start), axis=0), gext[full], 1, 1)
+        for c in range(2):
+
+            def both(product, at):
+                at = (at + c) * width
+                return product[at : at + width] + product[at + 2 * width : at + 3 * width]
+
+            def place(q):
+                return send1a.at[c, pl.ds(start * pad + q, width, stride=pad), :]
+
+            left = pltpu.roll(both(last, 0), early * room, 1)
+            for s in range(early):
+                coef = both(main, 4 * s)
+                for t in range(full):
+                    place(s * full + t)[...] = coef[:, t * LANES : (t + 1) * LANES]
+                term = coef[:, full * LANES :]
+                left = left + (pltpu.roll(term, s * room, 1) if s else term)
+            place(early * full)[...] = left
+        if block == 0:
+
+            @pl.when(hub)
+            def _():
+                pl.semaphore_wait(barrier, two - 1)
+                tell(other, me)
+
+            @pl.when(jnp.logical_not(hub))
+            def _():
+                pl.semaphore_wait(barrier, 1)
+
+        exchange(send1a, recv1a, early * full + 1, 0, block)
+
+    @pl.when(hub)
+    def _():
+        for copy in swaps:
+            copy.start()
+
     to_strips(send1b, coefficients(early, 0, full), 0)
     exchange(send1b, recv1b, full, 1)
 
@@ -326,19 +397,6 @@
     exchange(send2b, recv2b, full + 1, 3)
     for copy in returns:
         copy.start()
-    out = [
-        pltpu.make_async_copy(
-            uown.at[s], upd_hbm.at[s, pl.ds(var * lev, lev), 0], out_sem.at[s]
-        )
-        for s in range(slots)
-    ] + [
-        pltpu.make_async_copy(
-            urecv.at[s], upd_hbm.at[s, pl.ds(other * lev, lev), 0], out_sem.at[slots + s]
-        )
-        for s in range(slots)
-    ]
-    for copy in out[:slots]:
-        copy.start()
 
     def product(left, place):
         def on(here):
@@ -381,14 +439,27 @@
 
     for s in range(slots):
         returns[s].wait_recv()
-        out[slots + s].start()
     drain(send1a, early * full + 1, send_sem.at[0])
     drain(send1b, full, send_sem.at[1])
     drain(send2a, early * full, send_sem.at[2])
     drain(send2b, full + 1, send_sem.at[3])
     for copy in swaps + returns:
         copy.wait_send()
-    for copy in out:
+
+
+def place_results(own, back, rounded, upd, inc, upd_sem, inc_sem):
+    var = lax.axis_index("var")
+    slots, lev, _ = own.shape
+    copies = [
+        pltpu.make_async_copy(rounded.at[r], inc.at[r], inc_sem.at[r]) for r in range(inc.shape[0])
+    ]
+    for s in range(slots):
+        for at, (source, part) in enumerate(((own, var), (back, 1 - var))):
+            target = upd.at[s, pl.ds(part * lev, lev), 0]
+            copies.append(pltpu.make_async_copy(source.at[s], target, upd_sem.at[at, s]))
+    for copy in copies:
+        copy.start()
+    for copy in copies:
         copy.wait()
 
 
@@ -410,17 +481,18 @@
     square = pltpu.VMEM((lev, 1, lev), f32)
     dma = pltpu.SemaphoreType.DMA
     outside = functools.partial(pltpu.with_memory_space_constraint, memory_space=pltpu.HBM)
-    updated, increment = pl.pallas_call(
+    own, back, rounded = pl.pallas_call(
         functools.partial(kernel, n, slots, rows, lev, nn, lon),
         out_shape=(
-            jax.ShapeDtypeStruct((slots, 2 * lev, 1, nn), f32),
+            jax.ShapeDtypeStruct((slots, lev, nn), f32),
+            jax.ShapeDtypeStruct((slots, lev, nn), f32),
             jax.ShapeDtypeStruct((rows, lev, lon), bf16),
         ),
         in_specs=[
             hbm, hbm, hbm, hbm, hbm, hbm,
             pl.BlockSpec(memory_space=pltpu.SMEM), hbm,
         ],
-        out_specs=(anywhere, vmem),
+        out_specs=(vmem, vmem, vmem),
         scratch_shapes=[
             pltpu.VMEM((rows, lev, lon), bf16),
             pltpu.VMEM(((full + 1) * LANES, lon), f32),
@@ -448,13 +520,13 @@
             units,
             pltpu.VMEM((pair, nn), f32),
             pltpu.VMEM((pair, nn), f32),
-            units, units, units,
+            units,
             pltpu.VMEM(owner_slots.shape, jnp.int32),
             square, square, pltpu.VMEM((lev, lev), f32),
             dma((4,)),
             dma((1 + columns + 2 * slots,)),
             dma((4, 2)), dma((4, 2)), dma((4,)),
-            dma((3 + 2 * slots,)), dma((3 + 2 * slots,)), dma((2 * slots,)),
+            dma((3 + 2 * slots,)), dma((3 + 2 * slots,)),
         ],
         compiler_params=pltpu.CompilerParams(
             collective_id=0, has_side_effects=True, vmem_limit_bytes=48 * 1024 * 1024
@@ -470,6 +542,18 @@
         step_size,
         outside(owner_slots),
     )
+    updated, increment = pl.pallas_call(
+        place_results,
+        out_shape=(
+            jax.ShapeDtypeStruct((slots, 2 * lev, 1, nn), f32),
+            jax.ShapeDtypeStruct((rows, lev, lon), bf16),
+        ),
+        in_specs=[anywhere, anywhere, anywhere],
+        out_specs=(hbm, hbm),
+        scratch_shapes=[dma((2, slots)), dma((rows,))],
+        compiler_params=pltpu.CompilerParams(vmem_limit_bytes=1024 * 1024),
+        name="results",
+    )(own, back, rounded)
     return jnp.transpose(updated, (2, 0, 1, 3)), increment[None]
 
 

time: 91.5 us -> 87.9 us (0.961)
  local copies, waits for them, and re-layouts: 1.9 us -> 0 us
  Pallas kernels: 88.2 us -> 86.5 us
    pallas_call x1, Pallas kernels: 88.2 us -> 85.2 us  [local(): pl.pallas_call(functools.partial(kernel, n, slots, rows, lev, nn, lon), o...]
    unnamed x2 -> x0, local copies, waits for them, and re-layouts: 1.9 us -> none
    pallas_call x0 -> x1, Pallas kernels: none -> 1.37 us  [local(): pl.pallas_call(place_results, out_shape=(jax.ShapeDtypeStruct((slots, 2 *...]
where the time goes in v2:
time: 87.9 us; the launch traced here: 87.8 us
  Pallas kernels  86.5 us (98%)
  between operations  1.29 us (1%)
    pallas_call x1, Pallas kernels, local(): pl.pallas_call(functools.partial(kernel, n, slots, rows, lev, nn, lon), o...  85.2 us

profile of v2, /device:TPU:1, one launch (start us, length us, event | category | flops | bytes accessed | tf_op | source)
XLA Modules:
  0.0 87.8 jit_solution(6850374794681268219)
XLA Ops:
  1.3 85.2 %step.1 = (f32[3,70,384]{2,1,0:T(8,128)S(1)}, f32[3,70,384]{2,1,0:T(8,128)S(1)}, bf16[6,70,1536]{2,1,0:T(8,128)(2,1)S(1)}) custom-call(bf16[6,70,1536]{2,1,0:T(8,128)(2,1)} %bitcast.6, f32[70,1,70]{2,1,0:T(1,128)} %bitcast.8, f32[70,1,70]{2,1,0:T(1,128)} %bitcast.9, f32[70,70]{1,0:T(8,128)} %balance_hbm.1, f32[3,768,384]{2,1,0:T(8,128)} %leg_hbm.1, ...), custom_call_target="tpu_custom_call" | custom-call | tf_op jit(solution)/shard_map/step/pallas_call | solution.py:484
  86.5 1.4 %results.1 = (f32[3,140,1,384]{3,2,1,0:T(1,128)}, bf16[6,70,1536]{2,1,0:T(8,128)(2,1)}) custom-call(f32[3,70,384]{2,1,0:T(8,128)S(1)} %get-tuple-element.7.own, f32[3,70,384]{2,1,0:T(8,128)S(1)} %get-tuple-element.8.back, bf16[6,70,1536]{2,1,0:T(8,128)(2,1)S(1)} %get-tuple-element.9.rounded), custom_call_target="tpu_custom_call" | custom-call | tf_op jit(solution)/shard_map/results/pallas_call | solution.py:545
